TPU v7x, 256 devices: a whole 4x4x8 slice. The times are simulated.
256 devices in a mesh: grp: 4 (over y), dev: 64 (over x, z, core).
Axes of the slice: x: 4, y: 4, z: 8, core: 2. Of those that a mesh axis runs over, the one named last changes fastest.
Arguments:
- field: float32 [512, 512, 256, 4], P('dev', 'grp'), may hold values from -21 to 21
- start_basis: float32 [512, 64], replicated, may hold values from -6 to 6
Outputs:
- factor: float32 [512, 64], replicated
- core: float32 [64, 512, 256, 4], P(None, ('grp', 'dev'))
All inputs are finite; a program needn't handle non-finite values.
Results may differ from a plain program's by a relative error of at most 0.0003.
Values sent between devices are 32-bit elements; how exact they have to be, the bound alone decides.
No kernel may reach another device: no remote copies, remote signals or barrier semaphores. Data moves between devices by JAX's collectives and lax.ppermute only.
A program may use at most 192 MiB of HBM per device.

v0:
```python
import jax
import jax.numpy as jnp
from jax import lax
from jax.sharding import PartitionSpec as P

ITERS = 3


def product(left, right):
    return jnp.dot(left, right, precision=lax.Precision.HIGHEST, preferred_element_type=jnp.float32)


def on_device(field, start_basis):
    regrouped = lax.all_to_all(field, "dev", split_axis=1, concat_axis=0, tiled=True)
    rows = regrouped.shape[0]
    local_cols = regrouped.shape[1] * regrouped.shape[2] * regrouped.shape[3]
    unfold = regrouped.reshape(rows, local_cols)
    local_gram = product(unfold, unfold.T)
    gram = lax.psum(local_gram, ("grp", "dev"))
    basis = start_basis
    for step in range(ITERS):
        image = product(gram, basis)
        cross = product(image.T, image)
        chol = jnp.linalg.cholesky(cross)
        basis = lax.linalg.triangular_solve(
            chol, image, left_side=False, lower=True, transpose_a=True
        )
    core = product(basis.T, unfold)
    return (
        basis,
        core.reshape(basis.shape[1], regrouped.shape[1], regrouped.shape[2], regrouped.shape[3]),
    )


def solution(mesh):
    placed = (P("dev", "grp", None, None), P())
    return jax.shard_map(
        on_device,
        mesh=mesh,
        in_specs=placed,
        out_specs=(P(), P(None, ("grp", "dev"), None, None)),
        check_vma=False,
    )
```

profile of v0, /device:TPU:2, one launch (start us, length us, event | category | flops | bytes accessed | tf_op | source)
XLA Modules:
  0.0 543.9 jit_solution(3584140676412488919)
XLA Ops:
  7.2 0.0 copy-start
  7.2 0.0 all-reduce.2.cloned.1.call-start
  7.2 3.4 copy.14
  10.7 106.2 %all_to_all.15 = f32[8,128,256,4]{2,3,0,1:T(4,128)} all-to-all(f32[8,128,256,4]{2,3,0,1:T(4,128)S(1)} %copy.14), channel_id=1, replica_groups=mesh['grp'=4,'dev'=64] {'dev'}, dimensions={1} | all-to-all | bytes 8388608 | tf_op jit(solution)/shard_map/all_to_all | solution.py:14
  116.9 50.4 %copy.15 = f32[8,64,2,256,4]{0,1,4,3,2:T(8,128)} copy(f32[8,64,2,256,4]{3,4,0,2,1:T(4,128)} %bitcast.63) | data formatting | bytes 8388608 | tf_op jit(solution)/shard_map/all_to_all | solution.py:14
  167.2 48.3 %reshape.21 = f32[512,2048]{0,1:T(8,128)} reshape(f32[64,8,2,256,4]{1,0,4,3,2:T(8,128)} %bitcast.1) | data formatting | bytes 8388608 | tf_op jit(solution)/shard_map/reshape | solution.py:17
  215.5 11.3 %fusion.17 = f32[512,512]{1,0:T(8,128)} fusion(f32[512,2048]{0,1:T(8,128)} %reshape.21), kind=kOutput, calls=%fused_computation.31 | convolution fusion | flops 6442450944 | bytes 5242880 | tf_op jit(solution)/shard_map/dot_general | solution.py:10
  226.9 0.0 all-reduce.2.cloned.1.call-update
  226.9 5.2 dot_general.36
  232.1 252.3 %all-reduce.2.cloned.1.call-done = f32[512,512]{1,0:T(8,128)} async-done(((f32[512,512]{1,0:T(8,128)}), f32[512,512]{1,0:T(8,128)}) %all-reduce.2.cloned.1.call-update) | async-done | bytes 1048592 | tf_op jit(solution)/shard_map/psum | solution.py:19
  484.4 0.0 copy-done
  484.4 0.0 copy-start.1
  484.4 2.4 fusion.18
  486.9 0.3 fusion.19
  487.2 0.1 copy.16
  487.2 5.8 %cholesky.59 = f32[64,64]{1,0:T(8,128)S(1)} custom-call(f32[64,64]{1,0:T(8,128)S(1)} %fusion.12), custom_call_target="Cholesky" | custom-call | tf_op jit(solution)/shard_map/jit(cholesky)/cholesky | solution.py:24
  493.1 0.6 compare_reduce_fusion.2
  493.8 0.7 fusion.3
  494.4 4.9 custom-call.7
  499.3 0.3 convolution_bitcast_fusion.1
  499.7 2.4 fusion.20
  502.0 0.3 fusion.21
  502.3 0.1 copy.17
  502.4 5.8 %cholesky.70 = f32[64,64]{1,0:T(8,128)S(1)} custom-call(f32[64,64]{1,0:T(8,128)S(1)} %fusion.10), custom_call_target="Cholesky" | custom-call | tf_op jit(solution)/shard_map/jit(cholesky)/cholesky | solution.py:24
  508.3 0.6 compare_reduce_fusion.1
  508.9 0.7 fusion.4
  509.6 4.9 custom-call.8
  514.5 0.3 convolution_bitcast_fusion
  514.8 0.0 copy-done.1
  514.8 1.1 fusion.22
  516.0 0.3 fusion.23
  516.2 0.1 copy.18
  516.3 5.8 %cholesky.81 = f32[64,64]{1,0:T(8,128)S(1)} custom-call(f32[64,64]{1,0:T(8,128)S(1)} %fusion.8), custom_call_target="Cholesky" | custom-call | tf_op jit(solution)/shard_map/jit(cholesky)/cholesky | solution.py:24
  522.2 0.6 compare_reduce_fusion
  522.9 0.7 fusion.5
  523.5 4.9 custom-call.9
  528.4 0.3 fusion.6
  528.8 0.0 copy-start.2
  528.8 7.1 %fusion = f32[64,2,256,4]{2,0,3,1:T(8,128)S(1)} fusion(f32[2,256,4,512]{3,2,1,0:T(4,128)} %dot_general.36, f32[64,512]{1,0:T(8,128)S(1)} %fusion.6), kind=kOutput, calls=%fused_computation | convolution fusion | flops 805306368 | bytes 4849664 | tf_op jit(solution)/shard_map/dot_general | solution.py:10
  535.9 1.1 copy.20
  537.0 0.0 copy-done.2
  (6 shorter events, 0.1 us)
Async XLA Ops:
  7.2 477.3 %copy-start = (f32[512,64]{0,1:T(8,128)S(1)}, f32[512,64]{0,1:T(8,128)}, u32[]{:S(2)}) copy-start(f32[512,64]{0,1:T(8,128)} %param.6) | copy-start | bytes 393220
  7.2 477.3 %all-reduce.2.cloned.1.call-start = ((), (), s32[]{:S(2)}) async-start(), calls=%async_computation.1 | async-start | bytes 2097152 | tf_op jit(solution)/shard_map/psum | solution.py:19
  484.4 30.4 %copy-start.1 = (f32[512,512]{1,0:T(8,128)S(1)}, f32[512,512]{1,0:T(8,128)}, u32[]{:S(2)}) copy-start(f32[512,512]{1,0:T(8,128)} %all-reduce.2.cloned.1.call-done) | copy-start | bytes 3145732
  528.8 8.3 %copy-start.2 = (f32[64,512]{1,0:T(8,128)}, f32[64,512]{1,0:T(8,128)S(1)}, u32[]{:S(2)}) copy-start(f32[64,512]{1,0:T(8,128)S(1)} %fusion.6) | copy-start | bytes 393220
Sparse Core Ops, SparseCore 0:
  227.0 257.3 all-reduce.1
where the time goes:
time: 545 us; the launch traced here: 544 us
  waiting for transfers between devices  252 us (46%)
  local copies, waits for them, and re-layouts  109 us (20%)
  blocking collectives  106 us (19%)
  other arithmetic  36.2 us (7%)
  matrix products  26.2 us (5%)
  between operations  14.2 us (3%)
    psum x1, waiting for transfers between devices, on_device(): gram = lax.psum(local_gram, ('grp', 'dev'))  252 us
    all_to_all x1, blocking collectives, on_device(): lax.all_to_all(field, 'dev', split_axis=1, concat_axis=0, tiled=True)  106 us
    all_to_all x1, local copies, waits for them, and re-layouts, on_device(): lax.all_to_all(field, 'dev', split_axis=1, concat_axis=0, tiled=True)  50.4 us
    reshape x1, local copies, waits for them, and re-layouts, on_device(): unfold = regrouped.reshape(rows, local_cols)  48.3 us
    dot_general x8, matrix products, product(): jnp.dot(left, right, precision=lax.Precision.HIGHEST, preferred_element_t...  25.2 us
    another operation x9, other arithmetic, on_device(): chol = jnp.linalg.cholesky(cross)  19.6 us
    another operation x6, other arithmetic, on_device(): lax.linalg.triangular_solve(chol, image, left_side=False, lower=True, tra...  16.6 us
  transfers between devices with their start and end apart: 1, of which 1 were waited for; matrix products, arithmetic and copies ran while one was open for 1% of the time, Pallas kernels for 0%

commit v1 on v0

--- a/solution.py
+++ b/solution.py
@@ -16,7 +16,7 @@
     local_cols = regrouped.shape[1] * regrouped.shape[2] * regrouped.shape[3]
     unfold = regrouped.reshape(rows, local_cols)
     local_gram = product(unfold, unfold.T)
-    gram = lax.psum(local_gram, ("grp", "dev"))
+    gram = lax.psum(lax.psum(local_gram, "dev"), "grp")
     basis = start_basis
     for step in range(ITERS):
         image = product(gram, basis)

time: 545 us -> 524 us (0.961)
  waiting for transfers between devices: 252 us -> 231 us
    psum x1 -> x2, waiting for transfers between devices: 252 us -> 231 us  [on_device(): gram = lax.psum(lax.psum(local_gram, 'dev'), 'grp')]
  transfers between devices with their start and end apart: 1 -> 2, of which waited for: 1 -> 2; matrix products, arithmetic and copies ran while one was open for 1% -> 1% of each run, Pallas kernels for 0% -> 0%
where the time goes in v1:
time: 524 us; the launch traced here: 523 us
  waiting for transfers between devices  231 us (44%)
  local copies, waits for them, and re-layouts  109 us (21%)
  blocking collectives  106 us (20%)
  other arithmetic  36.2 us (7%)
  matrix products  26.1 us (5%)
  between operations  14.2 us (3%)
    psum x2, waiting for transfers between devices, on_device(): gram = lax.psum(lax.psum(local_gram, 'dev'), 'grp')  231 us
    all_to_all x1, blocking collectives, on_device(): lax.all_to_all(field, 'dev', split_axis=1, concat_axis=0, tiled=True)  106 us
    all_to_all x1, local copies, waits for them, and re-layouts, on_device(): lax.all_to_all(field, 'dev', split_axis=1, concat_axis=0, tiled=True)  50.4 us
    reshape x1, local copies, waits for them, and re-layouts, on_device(): unfold = regrouped.reshape(rows, local_cols)  48.3 us
    dot_general x8, matrix products, product(): jnp.dot(left, right, precision=lax.Precision.HIGHEST, preferred_element_t...  25.1 us
    another operation x9, other arithmetic, on_device(): chol = jnp.linalg.cholesky(cross)  19.6 us
    another operation x6, other arithmetic, on_device(): lax.linalg.triangular_solve(chol, image, left_side=False, lower=True, tra...  16.6 us
  transfers between devices with their start and end apart: 2, of which 2 were waited for; matrix products, arithmetic and copies ran while one was open for 1% of the time, Pallas kernels for 0%

profile of v1, /device:TPU:2, one launch (start us, length us, event | category | flops | bytes accessed | tf_op | source)
XLA Modules:
  0.0 523.0 jit_solution(11063321987038324154)
XLA Ops:
  7.2 0.0 copy-start
  7.2 0.0 all-reduce.3.cloned.1.call-start
  7.2 3.4 copy.14
  10.7 106.2 %all_to_all.15 = f32[8,128,256,4]{2,3,0,1:T(4,128)} all-to-all(f32[8,128,256,4]{2,3,0,1:T(4,128)S(1)} %copy.14), channel_id=1, replica_groups=mesh['grp'=4,'dev'=64] {'dev'}, dimensions={1} | all-to-all | bytes 8388608 | tf_op jit(solution)/shard_map/all_to_all | solution.py:14
  116.9 50.4 %copy.15 = f32[8,64,2,256,4]{0,1,4,3,2:T(8,128)} copy(f32[8,64,2,256,4]{3,4,0,2,1:T(4,128)} %bitcast.63) | data formatting | bytes 8388608 | tf_op jit(solution)/shard_map/all_to_all | solution.py:14
  167.2 48.3 %reshape.21 = f32[512,2048]{0,1:T(8,128)} reshape(f32[64,8,2,256,4]{1,0,4,3,2:T(8,128)} %bitcast.1) | data formatting | bytes 8388608 | tf_op jit(solution)/shard_map/reshape | solution.py:17
  215.5 11.3 %fusion.17 = f32[512,512]{1,0:T(8,128)} fusion(f32[512,2048]{0,1:T(8,128)} %reshape.21), kind=kOutput, calls=%fused_computation.31 | convolution fusion | flops 6442450944 | bytes 5242880 | tf_op jit(solution)/shard_map/dot_general | solution.py:10
  226.9 0.0 all-reduce.3.cloned.1.call-update
  226.9 0.0 all-reduce.5.cloned.1.call-start
  226.9 185.8 %all-reduce.3.cloned.1.call-done = f32[512,512]{1,0:T(8,128)} async-done(((f32[512,512]{1,0:T(8,128)}), f32[512,512]{1,0:T(8,128)}) %all-reduce.3.cloned.1.call-update) | async-done | bytes 1048592 | tf_op jit(solution)/shard_map/psum | solution.py:19
  412.8 0.0 all-reduce.5.cloned.1.call-update
  412.8 5.2 dot_general.36
  418.0 45.6 %all-reduce.5.cloned.1.call-done = f32[512,512]{1,0:T(8,128)} async-done(((f32[512,512]{1,0:T(8,128)}), f32[512,512]{1,0:T(8,128)}) %all-reduce.5.cloned.1.call-update) | async-done | bytes 1048592 | tf_op jit(solution)/shard_map/psum | solution.py:19
  463.6 0.0 copy-done
  463.6 0.0 copy-start.1
  463.6 2.4 fusion.18
  466.0 0.3 fusion.19
  466.3 0.1 copy.16
  466.4 5.8 %cholesky.59 = f32[64,64]{1,0:T(8,128)S(1)} custom-call(f32[64,64]{1,0:T(8,128)S(1)} %fusion.12), custom_call_target="Cholesky" | custom-call | tf_op jit(solution)/shard_map/jit(cholesky)/cholesky | solution.py:24
  472.3 0.6 compare_reduce_fusion.2
  472.9 0.7 fusion.3
  473.6 4.9 custom-call.7
  478.5 0.3 convolution_bitcast_fusion.1
  478.8 2.4 fusion.20
  481.2 0.3 fusion.21
  481.5 0.1 copy.17
  481.6 5.8 %cholesky.70 = f32[64,64]{1,0:T(8,128)S(1)} custom-call(f32[64,64]{1,0:T(8,128)S(1)} %fusion.10), custom_call_target="Cholesky" | custom-call | tf_op jit(solution)/shard_map/jit(cholesky)/cholesky | solution.py:24
  487.4 0.6 compare_reduce_fusion.1
  488.1 0.7 fusion.4
  488.7 4.9 custom-call.8
  493.6 0.3 convolution_bitcast_fusion
  494.0 0.0 copy-done.1
  494.0 1.1 fusion.22
  495.1 0.3 fusion.23
  495.4 0.1 copy.18
  495.5 5.8 %cholesky.81 = f32[64,64]{1,0:T(8,128)S(1)} custom-call(f32[64,64]{1,0:T(8,128)S(1)} %fusion.8), custom_call_target="Cholesky" | custom-call | tf_op jit(solution)/shard_map/jit(cholesky)/cholesky | solution.py:24
  501.4 0.6 compare_reduce_fusion
  502.0 0.7 fusion.5
  502.7 4.9 custom-call.9
  507.6 0.3 fusion.6
  507.9 0.0 copy-start.2
  507.9 7.1 %fusion = f32[64,2,256,4]{2,0,3,1:T(8,128)S(1)} fusion(f32[2,256,4,512]{3,2,1,0:T(4,128)} %dot_general.36, f32[64,512]{1,0:T(8,128)S(1)} %fusion.6), kind=kOutput, calls=%fused_computation | convolution fusion | flops 805306368 | bytes 4849664 | tf_op jit(solution)/shard_map/dot_general | solution.py:10
  515.0 1.1 copy.20
  516.2 0.0 copy-done.2
  (6 shorter events, 0.1 us)
Async XLA Ops:
  7.2 456.4 %copy-start = (f32[512,64]{0,1:T(8,128)S(1)}, f32[512,64]{0,1:T(8,128)}, u32[]{:S(2)}) copy-start(f32[512,64]{0,1:T(8,128)} %param.6) | copy-start | bytes 393220
  7.2 405.6 %all-reduce.3.cloned.1.call-start = ((), (), s32[]{:S(2)}) async-start(), calls=%async_computation.1 | async-start | bytes 2097152 | tf_op jit(solution)/shard_map/psum | solution.py:19
  226.9 236.7 %all-reduce.5.cloned.1.call-start = ((), (), s32[]{:S(2)}) async-start(), calls=%async_computation.2 | async-start | bytes 2097152 | tf_op jit(solution)/shard_map/psum | solution.py:19
  463.6 30.4 %copy-start.1 = (f32[512,512]{1,0:T(8,128)S(1)}, f32[512,512]{1,0:T(8,128)}, u32[]{:S(2)}) copy-start(f32[512,512]{1,0:T(8,128)} %all-reduce.5.cloned.1.call-done) | copy-start | bytes 3145732
  507.9 8.3 %copy-start.2 = (f32[64,512]{1,0:T(8,128)}, f32[64,512]{1,0:T(8,128)S(1)}, u32[]{:S(2)}) copy-start(f32[64,512]{1,0:T(8,128)S(1)} %fusion.6) | copy-start | bytes 393220
Sparse Core Ops, SparseCore 0:
  227.0 185.7 all-reduce.2
  415.1 48.4 all-reduce.4
